TPU v7x, 32 devices: a whole 2x2x4 slice. The times are simulated.
32 devices in a mesh: row: 8 (over y, x, core), col: 4 (over z).
Axes of the slice: x: 2, y: 2, z: 4, core: 2. Of those that a mesh axis runs over, the one named last changes fastest.
Arguments:
- col_samples: float32 [16, 2, 2048, 128], P('row', None, 'col'), may hold values from -6 to 6
- row_samples: float32 [16, 2, 128, 2048], P('row', None, None, 'col'), may hold values from -6 to 6
- pivot_rows: int32 [16, 128], P('row'), may hold values from 0 to 2047
- rank_blocks: int32 [16], P('row'), may hold values from 1 to 8
- upper_inverse: float32 [2, 2048, 2048], P(None, 'col', 'row'), as said below
- upanel_left: float32 [4, 2, 2048, 128], P('col'), may hold values from -0.125 to 0.125
Outputs:
- panel_right: float32 [16, 2, 128, 2048], P('row', None, None, 'col')
- cores: float32 [16, 4, 2, 128, 128], P('row', 'col')
Inputs may be any that keep to these rules, and one draw needn't show every extreme that they name: `rank_blocks`: the tile's rank is 16 times this. `upper_inverse`: zero below the diagonal in both parts.
All inputs are finite; a program needn't handle non-finite values.
Results may differ from a plain program's by a relative error of at most 0.00007.
Values sent between devices are 32-bit elements; how exact they have to be, the bound alone decides.
A program may use at most 64 MiB of HBM per device.

v0:
```python
import jax
import jax.numpy as jnp
from jax import lax
from jax.sharding import PartitionSpec as P

RANK_STEP = 16


def complex_product(pattern, left_real, left_imag, right_real, right_imag):

    def single(left, right):
        return jnp.einsum(
            pattern,
            left,
            right,
            precision=lax.Precision.HIGHEST,
            preferred_element_type=jnp.float32,
        )

    real_part = single(left_real, right_real) - single(left_imag, right_imag)
    imag_part = single(left_real, right_imag) + single(left_imag, right_real)
    return (real_part, imag_part)


def scale_rows(values, weight_real, weight_imag):
    wr = weight_real[:, :, None]
    wi = weight_imag[:, :, None]
    real_part = values[:, 0] * wr - values[:, 1] * wi
    imag_part = values[:, 0] * wi + values[:, 1] * wr
    return jnp.stack((real_part, imag_part), axis=1)


def on_device(col_samples, row_samples, pivot_rows, rank_blocks, upper_inverse, upanel_left):
    width_local = col_samples.shape[2]
    ranks_max = row_samples.shape[2]
    offset = lax.axis_index("col") * width_local
    positions = offset + lax.broadcasted_iota(jnp.int32, (1, 1, width_local), 2)
    hits = (pivot_rows[:, :, None] == positions).astype(jnp.float32)
    flipped = jnp.swapaxes(col_samples, 2, 3)
    partial_entries = jnp.sum(flipped * hits[:, None], axis=3)
    entries = lax.psum(partial_entries, "col")
    levels = lax.broadcasted_iota(jnp.int32, (1, ranks_max), 1)
    keeping = (levels < RANK_STEP * rank_blocks[:, None]).astype(jnp.float32)
    magnitude = jnp.maximum(entries[:, 0] * entries[:, 0] + entries[:, 1] * entries[:, 1], 1.0)
    factor_real = keeping * entries[:, 0] / magnitude
    factor_imag = -keeping * entries[:, 1] / magnitude
    scaled = scale_rows(row_samples, factor_real, factor_imag)
    portion = lax.all_gather(upper_inverse, "row", axis=2, tiled=True)
    real_part, imag_part = complex_product(
        "trk,kn->trn", scaled[:, 0], scaled[:, 1], portion[0], portion[1]
    )
    partial_panel = jnp.stack((real_part, imag_part), axis=1)
    panel_full = lax.psum(partial_panel, "col")
    core_real, core_imag = complex_product(
        "trn,jns->tjrs", panel_full[:, 0], panel_full[:, 1], upanel_left[:, 0], upanel_left[:, 1]
    )
    cores = jnp.stack((core_real, core_imag), axis=2)
    panel_local = lax.dynamic_slice_in_dim(panel_full, offset, width_local, 3)
    return (panel_local, cores)


def solution(mesh):
    in_specs = (
        P("row", None, "col", None),
        P("row", None, None, "col"),
        P("row", None),
        P("row"),
        P(None, "col", "row"),
        P("col", None, None, None),
    )
    out_specs = (P("row", None, None, "col"), P("row", "col", None, None, None))
    return jax.shard_map(
        on_device, mesh=mesh, in_specs=in_specs, out_specs=out_specs, check_vma=False
    )
```

profile of v0, /device:TPU:0, one launch (start us, length us, event | category | flops | bytes accessed | tf_op | source)
XLA Modules:
  0.0 263.2 jit_solution(7308855048611063219)
XLA Ops:
  7.2 0.0 all-gather.2.cloned.1.call-start
  7.2 0.7 all-gather.2.cloned.1.call-update
  7.9 0.0 all-reduce.2.cloned.1.call-start
  8.0 0.8 compare_convert_fusion
  8.8 0.0 copy-start.3
  8.8 1.4 fusion.20
  10.2 13.5 %psum.14 = f32[2,2,128]{2,1,0:T(2,128)S(1)} all-reduce(f32[2,2,128]{2,1,0:T(2,128)S(1)} %fusion.20), channel_id=1, replica_groups=mesh['row'=8,'col'=4] {'col'}, use_global_device_ids=true, to_apply=%region_1.0 | all-reduce | flops 512 | bytes 4096 | tf_op jit(solution)/shard_map/psum | solution.py:41
  23.7 0.7 broadcast_multiply_fusion
  24.3 0.1 select_divide_fusion
  24.4 44.1 %all-gather.2.cloned.1.call-done = f32[2,512,2048]{2,1,0:T(8,128)} async-done(((f32[2,512,256]{2,1,0:T(8,128)}), f32[2,512,2048]{2,1,0:T(8,128)}) %all-gather.2.cloned.1.call-update) | async-done | bytes 8388624 | tf_op jit(solution)/shard_map/all_gather | solution.py:48
  68.5 0.0 copy-start
  68.5 5.9 %fusion = f32[2,128,2048]{2,1,0:T(8,128)S(1)} fusion(f32[2,512,2048]{2,1,0:T(8,128)} %all-gather.2.cloned.1.call-done, f32[2,2,128,512]{3,2,1,0:T(8,128)} %param.7, f32[2,128]{1,0:T(2,128)S(1)} %get-tuple-element.7, f32[2,128]{1,0:T(2,128)S(1)} %get-tuple-element.6), kind=kOutput, calls=%fused_computation.3 | convolution fusion | flops 3221618688 | bytes 7342080 | tf_op jit(solution)/shard_map/trk,kn->trn/dot_general | solution.py:12
  74.4 0.0 copy-done.3
  74.4 5.7 %fusion.1 = f32[2,128,2048]{2,1,0:T(8,128)S(1)} fusion(f32[2,512,2048]{2,1,0:T(8,128)} %all-gather.2.cloned.1.call-done, f32[2,2,128,512]{3,2,1,0:T(8,128)S(1)} %copy-done.3, f32[2,128]{1,0:T(2,128)S(1)} %get-tuple-element.7, f32[2,128]{1,0:T(2,128)S(1)} %get-tuple-element.6), kind=kOutput, calls=%fused_computation.4 | convolution fusion | flops 3221618688 | bytes 7342080 | tf_op jit(solution)/shard_map/trk,kn->trn/dot_general | solution.py:12
  80.1 0.0 copy-done
  80.1 3.8 %fusion.7 = f32[2,1,128,2048]{3,2,0,1:T(8,128)S(1)} fusion(f32[2,128,2048]{2,1,0:T(8,128)S(1)} %fusion, f32[2,512,2048]{2,1,0:T(8,128)S(1)} %copy-done, f32[2,2,128,512]{3,2,1,0:T(8,128)S(1)} %copy-done.3, f32[2,128]{1,0:T(2,128)S(1)} %get-tuple-element.7, f32[2,128]{1,0:T(2,128)S(1)} %get-tuple-element.6), kind=kOutput, calls=%fused_computation.10 | convolution fusion | flops 3222142976 | bytes 9439232 | tf_op jit(solution)/shard_map/trk,kn->trn/dot_general | solution.py:12
  84.0 3.8 %fusion.5 = f32[2,1,128,2048]{3,2,0,1:T(8,128)S(1)} fusion(f32[2,128,2048]{2,1,0:T(8,128)S(1)} %fusion.1, f32[2,512,2048]{2,1,0:T(8,128)S(1)} %copy-done, f32[2,2,128,512]{3,2,1,0:T(8,128)S(1)} %copy-done.3, f32[2,128]{1,0:T(2,128)S(1)} %get-tuple-element.7, f32[2,128]{1,0:T(2,128)S(1)} %get-tuple-element.6), kind=kOutput, calls=%fused_computation.8 | convolution fusion | flops 3222142976 | bytes 9439232 | tf_op jit(solution)/shard_map/trk,kn->trn/dot_general | solution.py:12
  87.8 2.5 pad_maximum_fusion
  90.2 0.0 copy-start.2
  90.2 0.0 all-reduce.2.cloned.1.call-update
  90.3 155.1 %all-reduce.2.cloned.1.call-done = f32[2,2,128,2048]{3,2,0,1:T(8,128)} async-done(((f32[2,2,128,2048]{3,2,0,1:T(8,128)}), f32[2,2,128,2048]{3,2,0,1:T(8,128)}) %all-reduce.2.cloned.1.call-update) | async-done | bytes 4194320 | tf_op jit(solution)/shard_map/psum | solution.py:53
  245.4 0.0 copy-start.1
  245.4 1.4 constant_dynamic-slice_fusion
  246.8 1.0 copy.11
  247.9 0.0 copy-done.2
  247.9 0.1 copy-done.1
  248.0 1.8 fusion.8
  249.8 1.8 fusion.9
  251.7 2.1 fusion.15
  253.8 1.8 fusion.13
  255.6 0.7 copy.12
  (3 shorter events, 0.0 us)
Async XLA Ops:
  7.2 61.3 %all-gather.2.cloned.1.call-start = ((), (), s32[]{:S(2)}) async-start(), calls=%async_computation | async-start | bytes 9437184 | tf_op jit(solution)/shard_map/all_gather | solution.py:48
  7.9 237.5 %all-reduce.2.cloned.1.call-start = ((), (), s32[]{:S(2)}) async-start(), calls=%async_computation.1 | async-start | bytes 8388608 | tf_op jit(solution)/shard_map/psum | solution.py:53
  8.8 65.6 %copy-start.3 = (f32[2,2,128,512]{3,2,1,0:T(8,128)S(1)}, f32[2,2,128,512]{3,2,1,0:T(8,128)}, u32[]{:S(2)}) copy-start(f32[2,2,128,512]{3,2,1,0:T(8,128)} %param.7) | copy-start | bytes 3145732
  68.5 11.7 %copy-start = (f32[2,512,2048]{2,1,0:T(8,128)S(1)}, f32[2,512,2048]{2,1,0:T(8,128)}, u32[]{:S(2)}) copy-start(f32[2,512,2048]{2,1,0:T(8,128)} %all-gather.2.cloned.1.call-done) | copy-start | bytes 25165828
  90.2 157.6 %copy-start.2 = (f32[1,2,2048,128]{3,2,1,0:T(8,128)S(1)}, f32[1,2,2048,128]{3,2,1,0:T(8,128)}, u32[]{:S(2)}) copy-start(f32[1,2,2048,128]{3,2,1,0:T(8,128)} %param.11) | copy-start | bytes 6291460
  245.4 2.6 copy-start.1
Sparse Core Ops, SparseCore 0:
  9.8 58.5 all-gather.1
  90.4 154.9 all-reduce.1
where the time goes:
time: 263 us
  waiting for transfers between devices  200 us (76%)
  matrix products  26.8 us (10%)
  between operations  14.2 us (5%)
  blocking collectives  13.5 us (5%)
  other arithmetic  5.43 us (2%)
  local copies, waits for them, and re-layouts  3.36 us (1%)
    psum x1, waiting for transfers between devices, on_device(): panel_full = lax.psum(partial_panel, 'col')  155 us
    all_gather x1, waiting for transfers between devices, on_device(): portion = lax.all_gather(upper_inverse, 'row', axis=2, tiled=True)  44.1 us
    dot_general x8, matrix products, single(): jnp.einsum(pattern, left, right, precision=lax.Precision.HIGHEST, preferr...  26.8 us
    psum x1, blocking collectives, on_device(): entries = lax.psum(partial_entries, 'col')  13.5 us
  transfers between devices with their start and end apart: 2, of which 2 were waited for; matrix products, arithmetic and copies ran while one was open for 1% of the time, Pallas kernels for 0%

commit v1 on v0

--- a/solution.py
+++ b/solution.py
@@ -50,7 +50,11 @@
         "trk,kn->trn", scaled[:, 0], scaled[:, 1], portion[0], portion[1]
     )
     partial_panel = jnp.stack((real_part, imag_part), axis=1)
-    panel_full = lax.psum(partial_panel, "col")
+    panel_full = partial_panel
+    for hop in (1, 2):
+        panel_full = panel_full + lax.ppermute(
+            panel_full, "col", [(dev, dev ^ hop) for dev in range(4)]
+        )
     core_real, core_imag = complex_product(
         "trn,jns->tjrs", panel_full[:, 0], panel_full[:, 1], upanel_left[:, 0], upanel_left[:, 1]
     )

time: 263 us -> 389 us (1.48)
  waiting for transfers between devices: 200 us -> 317 us
  other arithmetic: 5.43 us -> 11.9 us
  starting transfers between devices: 0.08 us -> 4 us
    ppermute x0 -> x2, waiting for transfers between devices: none -> 272 us  [on_device(): lax.ppermute(panel_full, 'col', [(dev, dev ^ hop) for dev in range(4)])]
    psum x1 -> x0, waiting for transfers between devices: 155 us -> none  [on_device(): panel_full = lax.psum(partial_panel, 'col')]
    add x0 -> x2, other arithmetic: none -> 8.52 us  [on_device(): panel_full + lax.ppermute(panel_full, 'col', [(dev, dev ^ hop) for dev in...]
    ppermute x0 -> x2, starting transfers between devices: none -> 3.96 us  [on_device(): lax.ppermute(panel_full, 'col', [(dev, dev ^ hop) for dev in range(4)])]
  transfers between devices with their start and end apart: 2 -> 3, of which waited for: 2 -> 3; matrix products, arithmetic and copies ran while one was open for 1% -> 1% of each run, Pallas kernels for 0% -> 0%
where the time goes in v1:
time: 389 us
  waiting for transfers between devices  317 us (81%)
  matrix products  26.8 us (7%)
  between operations  14.2 us (4%)
  blocking collectives  13.5 us (3%)
  other arithmetic  11.9 us (3%)
  starting transfers between devices  4 us (1%)
    ppermute x2, waiting for transfers between devices, on_device(): lax.ppermute(panel_full, 'col', [(dev, dev ^ hop) for dev in range(4)])  272 us
    all_gather x1, waiting for transfers between devices, on_device(): portion = lax.all_gather(upper_inverse, 'row', axis=2, tiled=True)  44.1 us
    dot_general x8, matrix products, single(): jnp.einsum(pattern, left, right, precision=lax.Precision.HIGHEST, preferr...  26.8 us
    psum x1, blocking collectives, on_device(): entries = lax.psum(partial_entries, 'col')  13.5 us
    add x2, other arithmetic, on_device(): panel_full + lax.ppermute(panel_full, 'col', [(dev, dev ^ hop) for dev in...  8.52 us
  transfers between devices with their start and end apart: 3, of which 3 were waited for; matrix products, arithmetic and copies ran while one was open for 1% of the time, Pallas kernels for 0%

profile of v1, /device:TPU:0, one launch (start us, length us, event | category | flops | bytes accessed | tf_op | source)
XLA Modules:
  0.0 388.8 jit_solution(2393113915347066796)
XLA Ops:
  7.2 0.0 all-gather.2.cloned.1.call-start
  7.2 0.7 all-gather.2.cloned.1.call-update
  7.9 0.8 compare_convert_fusion
  8.7 0.0 copy-start.4
  8.7 1.4 fusion.20
  10.1 13.5 %psum.7 = f32[2,2,128]{2,1,0:T(2,128)S(1)} all-reduce(f32[2,2,128]{2,1,0:T(2,128)S(1)} %fusion.20), channel_id=1, replica_groups=mesh['row'=8,'col'=4] {'col'}, use_global_device_ids=true, to_apply=%region_1.0 | all-reduce | flops 512 | bytes 4096 | tf_op jit(solution)/shard_map/psum | solution.py:41
  23.6 0.7 broadcast_multiply_fusion
  24.3 0.1 select_divide_fusion
  24.4 44.1 %all-gather.2.cloned.1.call-done = f32[2,512,2048]{2,1,0:T(8,128)} async-done(((f32[2,512,256]{2,1,0:T(8,128)}), f32[2,512,2048]{2,1,0:T(8,128)}) %all-gather.2.cloned.1.call-update) | async-done | bytes 8388624 | tf_op jit(solution)/shard_map/all_gather | solution.py:48
  68.5 5.9 %fusion = f32[2,128,2048]{2,1,0:T(8,128)S(1)} fusion(f32[2,512,2048]{2,1,0:T(8,128)} %all-gather.2.cloned.1.call-done, f32[2,2,128,512]{3,2,1,0:T(8,128)} %param.7, f32[2,128]{1,0:T(2,128)S(1)} %get-tuple-element.7, f32[2,128]{1,0:T(2,128)S(1)} %get-tuple-element.6), kind=kOutput, calls=%fused_computation.3 | convolution fusion | flops 3221618688 | bytes 7342080 | tf_op jit(solution)/shard_map/trk,kn->trn/dot_general | solution.py:12
  74.4 0.0 copy-done.4
  74.4 5.7 %fusion.1 = f32[2,128,2048]{2,1,0:T(8,128)S(1)} fusion(f32[2,512,2048]{2,1,0:T(8,128)} %all-gather.2.cloned.1.call-done, f32[2,2,128,512]{3,2,1,0:T(8,128)S(1)} %copy-done.4, f32[2,128]{1,0:T(2,128)S(1)} %get-tuple-element.7, f32[2,128]{1,0:T(2,128)S(1)} %get-tuple-element.6), kind=kOutput, calls=%fused_computation.4 | convolution fusion | flops 3221618688 | bytes 7342080 | tf_op jit(solution)/shard_map/trk,kn->trn/dot_general | solution.py:12
  80.1 0.0 copy-done
  80.1 3.8 fusion.7
  83.9 3.8 fusion.5
  87.7 0.0 copy-start.1
  87.8 0.4 pad_maximum_fusion
  88.1 1.6 collective-permute-start
  89.7 91.2 %collective-permute-done = f32[2,2,128,2048]{3,2,0,1:T(8,128)S(1)} collective-permute-done((f32[2,2,128,2048]{3,2,0,1:T(8,128)S(1)}, f32[2,2,128,2048]{3,2,0,1:T(8,128)S(1)}, u32[]{:S(2)}, u32[]{:S(2)}) %collective-permute-start) | collective-permute-done | bytes 4194336 | tf_op jit(solution)/shard_map/ppermute | solution.py:55
  180.9 3.1 fusion.29
  184.1 0.0 copy-done.1
  184.1 0.1 copy-done.2
  184.2 2.4 collective-permute-start.1
  186.6 180.6 %collective-permute-done.1 = f32[2,2,128,2048]{3,2,0,1:T(8,128)} collective-permute-done((f32[2,2,128,2048]{3,2,0,1:T(8,128)}, f32[2,2,128,2048]{3,2,0,1:T(8,128)}, u32[]{:S(2)}, u32[]{:S(2)}) %collective-permute-start.1) | collective-permute-done | bytes 4194336 | tf_op jit(solution)/shard_map/ppermute | solution.py:55
  367.1 5.4 %fusion.31 = f32[2,2,128,2048]{3,2,0,1:T(8,128)S(1)} fusion(f32[2,2,128,2048]{3,2,0,1:T(8,128)} %collective-permute-done.1, f32[2,2,128,2048]{3,2,0,1:T(8,128)} %copy-done.2, f32[2,1,128,2048]{3,2,0,1:T(8,128)S(1)} %fusion.7, f32[2,1,128,2048]{3,2,0,1:T(8,128)} %copy-done.1), kind=kLoop, calls=%fused_computation.48 | loop fusion | flops 3145728 | bytes 16777216 | tf_op jit(solution)/shard_map/add | solution.py:55
  372.5 1.8 fusion.10
  374.4 2.1 fusion.11
  376.4 1.8 fusion.15
  378.3 1.8 fusion.13
  380.1 0.1 constant_dynamic-slice_fusion
  380.2 1.0 copy.11
  381.3 0.7 copy.12
  (7 shorter events, 0.0 us)
Async XLA Ops:
  7.2 61.3 %all-gather.2.cloned.1.call-start = ((), (), s32[]{:S(2)}) async-start(), calls=%async_computation | async-start | bytes 9437184 | tf_op jit(solution)/shard_map/all_gather | solution.py:48
  8.7 65.7 %copy-start.4 = (f32[2,2,128,512]{3,2,1,0:T(8,128)S(1)}, f32[2,2,128,512]{3,2,1,0:T(8,128)}, u32[]{:S(2)}) copy-start(f32[2,2,128,512]{3,2,1,0:T(8,128)} %param.7) | copy-start | bytes 3145732
  68.5 11.7 %copy-start = (f32[2,512,2048]{2,1,0:T(8,128)S(1)}, f32[2,512,2048]{2,1,0:T(8,128)}, u32[]{:S(2)}) copy-start(f32[2,512,2048]{2,1,0:T(8,128)} %all-gather.2.cloned.1.call-done) | copy-start | bytes 25165828
  87.7 96.3 %copy-start.1 = (f32[2,1,128,2048]{3,2,0,1:T(8,128)}, f32[2,1,128,2048]{3,2,0,1:T(8,128)S(1)}, u32[]{:S(2)}) copy-start(f32[2,1,128,2048]{3,2,0,1:T(8,128)S(1)} %fusion.5) | copy-start | bytes 6291460
  88.1 92.8 %collective-permute-start = (f32[2,2,128,2048]{3,2,0,1:T(8,128)S(1)}, f32[2,2,128,2048]{3,2,0,1:T(8,128)S(1)}, u32[]{:S(2)}, u32[]{:S(2)}) collective-permute-start(f32[2,2,128,2048]{3,2,0,1:T(8,128)S(1)} %pad_maximum_fusion), channel_id=1, source_target_pairs={{0,1},{1,0},{2,3},{3,2},{4,5},{5,4},{6,7},{7,6},{8,9},{9,8},{10,11... | collective-permute-start | bytes 12582920 | tf_op jit(solution)/shard_map/ppermute | solution.py:55
  180.9 3.2 copy-start.2
  184.2 183.0 %collective-permute-start.1 = (f32[2,2,128,2048]{3,2,0,1:T(8,128)}, f32[2,2,128,2048]{3,2,0,1:T(8,128)}, u32[]{:S(2)}, u32[]{:S(2)}) collective-permute-start(f32[2,2,128,2048]{3,2,0,1:T(8,128)} %fusion.29), channel_id=1, source_target_pairs={{0,2},{1,3},{2,0},{3,1},{4,6},{5,7},{6,4},{7,5},{8,10},{9,11},{10,... | collective-permute-start | bytes 12582920 | tf_op jit(solution)/shard_map/ppermute | solution.py:55
  186.6 186.0 %copy-start.3 = (f32[1,2,2048,128]{3,2,1,0:T(8,128)S(1)}, f32[1,2,2048,128]{3,2,1,0:T(8,128)}, u32[]{:S(2)}) copy-start(f32[1,2,2048,128]{3,2,1,0:T(8,128)} %param.11) | copy-start | bytes 6291460
Sparse Core Ops, SparseCore 0:
  9.8 58.5 all-gather.1

commit v2 on v0

--- a/solution.py
+++ b/solution.py
@@ -45,7 +45,7 @@
     factor_real = keeping * entries[:, 0] / magnitude
     factor_imag = -keeping * entries[:, 1] / magnitude
     scaled = scale_rows(row_samples, factor_real, factor_imag)
-    portion = lax.all_gather(upper_inverse, "row", axis=2, tiled=True)
+    portion = jnp.concatenate(lax.all_gather(upper_inverse, "row"), axis=2)
     real_part, imag_part = complex_product(
         "trk,kn->trn", scaled[:, 0], scaled[:, 1], portion[0], portion[1]
     )

time: 263 us -> 282 us (1.072)
  local copies, waits for them, and re-layouts: 3.36 us -> 25.3 us
    squeeze x0 -> x2, local copies, waits for them, and re-layouts: none -> 9.85 us  [the longest x1 4.98 us: on_device(): portion[0]]
    all_gather x0 -> x1, local copies, waits for them, and re-layouts: none -> 8.24 us  [on_device(): portion = jnp.concatenate(lax.all_gather(upper_inverse, 'row'), axis=2)]
    slice x0 -> x1, local copies, waits for them, and re-layouts: none -> 3.81 us  [on_device(): portion[0]]
where the time goes in v2:
time: 282 us
  waiting for transfers between devices  198 us (70%)
  local copies, waits for them, and re-layouts  25.3 us (9%)
  matrix products  24.8 us (9%)
  between operations  14.2 us (5%)
  blocking collectives  13.5 us (5%)
  other arithmetic  5.35 us (2%)
    psum x1, waiting for transfers between devices, on_device(): panel_full = lax.psum(partial_panel, 'col')  155 us
    all_gather x1, waiting for transfers between devices, on_device(): portion = jnp.concatenate(lax.all_gather(upper_inverse, 'row'), axis=2)  42.6 us
    dot_general x8, matrix products, single(): jnp.einsum(pattern, left, right, precision=lax.Precision.HIGHEST, preferr...  24.8 us
    psum x1, blocking collectives, on_device(): entries = lax.psum(partial_entries, 'col')  13.5 us
    all_gather x1, local copies, waits for them, and re-layouts, on_device(): portion = jnp.concatenate(lax.all_gather(upper_inverse, 'row'), axis=2)  8.24 us
  transfers between devices with their start and end apart: 2, of which 2 were waited for; matrix products, arithmetic and copies ran while one was open for 1% of the time, Pallas kernels for 0%

profile of v2, /device:TPU:0, one launch (start us, length us, event | category | flops | bytes accessed | tf_op | source)
XLA Modules:
  0.0 281.5 jit_solution(16148595749896217609)
XLA Ops:
  7.2 0.0 all-gather.3.cloned.1.call-start
  7.2 0.7 all-gather.3.cloned.1.call-update
  7.9 0.0 all-reduce.2.cloned.1.call-start
  8.0 0.8 compare_convert_fusion
  8.8 1.3 fusion.14
  10.1 13.5 %psum.14 = f32[2,2,128]{2,1,0:T(2,128)S(1)} all-reduce(f32[2,2,128]{2,1,0:T(2,128)S(1)} %fusion.14), channel_id=1, replica_groups=mesh['row'=8,'col'=4] {'col'}, use_global_device_ids=true, to_apply=%region_1.0 | all-reduce | flops 512 | bytes 4096 | tf_op jit(solution)/shard_map/psum | solution.py:41
  23.6 0.7 broadcast_multiply_fusion
  24.2 0.1 select_divide_fusion
  24.3 42.6 %all-gather.3.cloned.1.call-done = f32[16,512,256]{2,1,0:T(8,128)} async-done(((f32[2,512,256]{2,1,0:T(8,128)}), f32[16,512,256]{2,1,0:T(8,128)}) %all-gather.3.cloned.1.call-update) | async-done | bytes 8388624 | tf_op jit(solution)/shard_map/all_gather | solution.py:48
  66.9 8.2 %copy.17 = f32[8,2,512,256]{3,0,2,1:T(8,128)S(1)} copy(f32[8,2,512,256]{3,2,1,0:T(8,128)} %bitcast.81) | data formatting | bytes 16777216 | tf_op jit(solution)/shard_map/all_gather | solution.py:48
  75.1 3.8 %fusion.25 = (f32[1,512,8,256]{3,2,1,0:T(8,128)}, f32[1,512,8,256]{3,2,1,0:T(8,128)}) fusion(f32[2,512,8,256]{3,2,1,0:T(8,128)S(1)} %bitcast.80), kind=kLoop, calls=%fused_computation.43 | loop fusion | bytes 16777216 | tf_op jit(solution)/shard_map/slice | solution.py:50
  78.9 4.9 %reshape.116 = f32[512,2048,1]{1,0,2:T(8,128)} reshape(f32[1,512,8,256]{3,2,1,0:T(8,128)} %get-tuple-element.7) | data formatting | bytes 8388608 | tf_op jit(solution)/shard_map/squeeze | solution.py:50
  83.8 5.0 %reshape.115 = f32[512,2048,1]{1,0,2:T(8,128)} reshape(f32[1,512,8,256]{3,2,1,0:T(8,128)} %get-tuple-element.6) | data formatting | bytes 8388608 | tf_op jit(solution)/shard_map/squeeze | solution.py:50
  88.8 0.0 copy-done.4
  88.8 5.8 %fusion.21 = f32[2,128,2048]{2,1,0:T(8,128)S(1)} fusion(f32[512,2048,1]{1,0,2:T(8,128)} %reshape.116, f32[2,2,128,512]{3,2,1,0:T(8,128)S(1)} %copy-done.4, f32[2,128]{1,0:T(2,128)S(1)} %get-tuple-element.9, f32[2,128]{1,0:T(2,128)S(1)} %get-tuple-element.8), kind=kOutput, calls=%fused_computation.28 | convolution fusion | flops 3221618688 | bytes 7342080 | tf_op jit(solution)/shard_map/trk,kn->trn/dot_general | solution.py:12
  94.6 0.0 copy-done.1
  94.6 3.8 %fusion.23 = f32[2,128,2048]{2,1,0:T(8,128)S(1)} fusion(f32[512,2048,1]{1,0,2:T(8,128)S(1)} %copy-done.1, f32[2,2,128,512]{3,2,1,0:T(8,128)S(1)} %copy-done.4, f32[2,128]{1,0:T(2,128)S(1)} %get-tuple-element.9, f32[2,128]{1,0:T(2,128)S(1)} %get-tuple-element.8), kind=kOutput, calls=%fused_computation.30 | convolution fusion | flops 3221618688 | bytes 7342080 | tf_op jit(solution)/shard_map/trk,kn->trn/dot_general | solution.py:12
  98.4 0.0 copy-start
  98.4 3.8 %fusion = f32[2,1,128,2048]{3,2,0,1:T(8,128)S(1)} fusion(f32[2,128,2048]{2,1,0:T(8,128)S(1)} %fusion.21, f32[512,2048,1]{1,0,2:T(8,128)S(1)} %copy-done.1, f32[2,2,128,512]{3,2,1,0:T(8,128)S(1)} %copy-done.4, f32[2,128]{1,0:T(2,128)S(1)} %get-tuple-element.9, f32[2,128]{1,0:T(2,128)S(1)} %get-tuple-element.8), kind=kOutput, calls=%fused_computation.3 | convolution fusion | flops 3222142976 | bytes 9439232 | tf_op jit(solution)/shard_map/trk,kn->trn/dot_general | solution.py:12
  102.2 0.0 copy-done
  102.3 3.8 %fusion.1 = f32[2,1,128,2048]{3,2,0,1:T(8,128)S(1)} fusion(f32[2,128,2048]{2,1,0:T(8,128)S(1)} %fusion.23, f32[512,2048,1]{1,0,2:T(8,128)S(1)} %copy-done, f32[2,2,128,512]{3,2,1,0:T(8,128)S(1)} %copy-done.4, f32[2,128]{1,0:T(2,128)S(1)} %get-tuple-element.9, f32[2,128]{1,0:T(2,128)S(1)} %get-tuple-element.8), kind=kOutput, calls=%fused_computation.5 | convolution fusion | flops 3222142976 | bytes 9439232 | tf_op jit(solution)/shard_map/trk,kn->trn/dot_general | solution.py:12
  106.1 2.5 pad_maximum_fusion
  108.6 0.0 all-reduce.2.cloned.1.call-update
  108.6 155.1 %all-reduce.2.cloned.1.call-done = f32[2,2,128,2048]{3,2,0,1:T(8,128)} async-done(((f32[2,2,128,2048]{3,2,0,1:T(8,128)}), f32[2,2,128,2048]{3,2,0,1:T(8,128)}) %all-reduce.2.cloned.1.call-update) | async-done | bytes 4194320 | tf_op jit(solution)/shard_map/psum | solution.py:53
  263.7 1.4 constant_dynamic-slice_fusion
  265.2 1.0 copy.13
  266.2 0.1 copy-done.2
  266.3 2.1 fusion.2
  268.4 1.8 fusion.3
  270.2 1.9 fusion.9
  272.1 1.8 fusion.7
  274.0 0.7 copy.14
  (8 shorter events, 0.0 us)
Async XLA Ops:
  7.2 59.7 %all-gather.3.cloned.1.call-start = ((), (), s32[]{:S(2)}) async-start(), calls=%async_computation.1 | async-start | bytes 9437184 | tf_op jit(solution)/shard_map/all_gather | solution.py:48
  7.9 255.8 %all-reduce.2.cloned.1.call-start = ((), (), s32[]{:S(2)}) async-start(), calls=%async_computation | async-start | bytes 8388608 | tf_op jit(solution)/shard_map/psum | solution.py:53
  83.8 5.0 %copy-start.4 = (f32[2,2,128,512]{3,2,1,0:T(8,128)S(1)}, f32[2,2,128,512]{3,2,1,0:T(8,128)}, u32[]{:S(2)}) copy-start(f32[2,2,128,512]{3,2,1,0:T(8,128)} %param.7) | copy-start | bytes 3145732
  88.8 5.9 %copy-start.1 = (f32[512,2048,1]{1,0,2:T(8,128)S(1)}, f32[512,2048,1]{1,0,2:T(8,128)}, u32[]{:S(2)}) copy-start(f32[512,2048,1]{1,0,2:T(8,128)} %reshape.115) | copy-start | bytes 12582916
  98.4 3.8 %copy-start = (f32[512,2048,1]{1,0,2:T(8,128)S(1)}, f32[512,2048,1]{1,0,2:T(8,128)}, u32[]{:S(2)}) copy-start(f32[512,2048,1]{1,0,2:T(8,128)} %reshape.116) | copy-start | bytes 12582916
  108.5 157.6 %copy-start.3 = (f32[1,2,2048,128]{3,2,1,0:T(8,128)S(1)}, f32[1,2,2048,128]{3,2,1,0:T(8,128)}, u32[]{:S(2)}) copy-start(f32[1,2,2048,128]{3,2,1,0:T(8,128)} %param.11) | copy-start | bytes 6291460
  263.7 2.6 copy-start.2
Sparse Core Ops, SparseCore 0:
  9.9 56.9 all-gather.2
  108.7 154.9 all-reduce.1
